TPU v7x, 32 devices: a whole 2x2x4 slice. The times are simulated.
32 devices in a mesh: gx: 16 (over z, y, x), gy: 2 (over core).
Axes of the slice: x: 2, y: 2, z: 4, core: 2. Of those that a mesh axis runs over, the one named last changes fastest.
Arguments:
- displacement: float32 [3, 32, 128, 256], P(None, None, 'gx', 'gy'), may hold values from -6 to 6
- velocity: float32 [3, 32, 128, 256], P(None, None, 'gx', 'gy'), may hold values from -6 to 6
- slopes: float32 [2, 32, 128, 256], P(None, None, 'gx', 'gy'), may hold values from -0.5 to 0.5
- stretch: float32 [32, 128, 256], P(None, 'gx', 'gy'), may hold values from 0.6 to 1.4
- moduli: float32 [2, 32, 128, 256], P(None, None, 'gx', 'gy'), may hold values from 0.3 to 1
- buoyancy: float32 [32, 128, 256], P(None, 'gx', 'gy'), may hold values from 0.5 to 1.5
- probes: float32 [4, 128, 128], P(None, 'gy'), may hold values from -0.0048828125 to 0.0048828125
Outputs:
- final_displacement: float32 [3, 32, 128, 256], P(None, None, 'gx', 'gy')
- basis: float32 [64, 48, 128], P('gx', 'gy')
- factor: float32 [128, 128], replicated
All inputs are finite; a program needn't handle non-finite values.
Results may differ from a plain program's by a relative error of at most 0.0003.
Values sent between devices are 32-bit elements; how exact they have to be, the bound alone decides.
No kernel may reach another device: no remote copies, remote signals or barrier semaphores. Data moves between devices by JAX's collectives and lax.ppermute only.
A program may use at most 64 MiB of HBM per device.

v0:
```python
import math
import jax
import jax.numpy as jnp
from jax import lax
from jax.sharding import PartitionSpec as P

STEPS = 4
time_step = 0.12


def extended(block, sides, width):
    for axis, dim in sides:
        count = lax.axis_size(axis)
        forward = [(i, i + 1) for i in range(count - 1)]
        backward = [(target, source) for source, target in forward]
        low = lax.ppermute(
            lax.slice_in_dim(block, block.shape[dim] - width, None, axis=dim), axis, forward
        )
        high = lax.ppermute(lax.slice_in_dim(block, 0, width, axis=dim), axis, backward)
        block = jnp.concatenate([low, block, high], axis=dim)
    return block


def fourth(values, dimension):
    length_out = values.shape[dimension] - 4

    def segment(offset):
        return lax.slice_in_dim(values, offset, offset + length_out, axis=dimension)

    return (segment(0) - segment(4) + 8.0 * (segment(3) - segment(1))) / 12.0


def vertical(values):
    padded = jnp.pad(values, ((0, 0), (2, 2), (0, 0), (0, 0)))
    return fourth(padded, 1)


def gradient(padded, slope_x, slope_y, stretch):
    d_x = fourth(padded[:, :, :, 2:-2], 2)
    d_y = fourth(padded[:, :, 2:-2, :], 3)
    d_r = vertical(padded[:, :, 2:-2, 2:-2])
    return jnp.stack([d_x + slope_x * d_r, d_y + slope_y * d_r, stretch * d_r], axis=1)


def stresses(gradients, lame, shear):
    divergence = gradients[0, 0] + gradients[1, 1] + gradients[2, 2]
    pressure = lame * divergence
    return jnp.stack(
        [
            pressure + 2.0 * shear * gradients[0, 0],
            pressure + 2.0 * shear * gradients[1, 1],
            pressure + 2.0 * shear * gradients[2, 2],
            shear * (gradients[0, 1] + gradients[1, 0]),
            shear * (gradients[0, 2] + gradients[2, 0]),
            shear * (gradients[1, 2] + gradients[2, 1]),
        ]
    )


def forces(padded, slope_x, slope_y, stretch):
    d_x = fourth(padded[:, :, :, 2:-2], 2)
    d_y = fourth(padded[:, :, 2:-2, :], 3)
    d_r = vertical(padded[:, :, 2:-2, 2:-2])
    rows_x = (0, 3, 4)
    rows_y = (3, 1, 5)
    rows_z = (4, 5, 2)
    return jnp.stack(
        [
            d_x[rows_x[component]]
            + slope_x * d_r[rows_x[component]]
            + d_y[rows_y[component]]
            + slope_y * d_r[rows_y[component]]
            + stretch * d_r[rows_z[component]]
            for component in range(3)
        ]
    )


def lower_factor(gram):
    order = gram.shape[0]
    positions = jnp.arange(order, dtype=jnp.int32)

    def column_step(column_index, lower):
        picker = (positions == column_index).astype(jnp.float32)
        column = jnp.dot(gram, picker, precision=lax.Precision.HIGHEST)
        row_of = jnp.dot(picker, lower, precision=lax.Precision.HIGHEST)
        column = column - jnp.dot(lower, row_of, precision=lax.Precision.HIGHEST)
        pivot = jnp.sqrt(jnp.sum(column * picker))
        entries = jnp.where(
            positions > column_index,
            column / pivot,
            jnp.where(positions == column_index, pivot, 0.0),
        )
        return lower + entries[:, None] * picker[None, :]

    return lax.fori_loop(0, order, column_step, jnp.zeros_like(gram))


def lower_inverse(lower):
    order = lower.shape[0]
    positions = jnp.arange(order, dtype=jnp.int32)

    def row_step(row_index, inverse):
        picker = (positions == row_index).astype(jnp.float32)
        row_of = jnp.dot(picker, lower, precision=lax.Precision.HIGHEST)
        pivot = jnp.sum(row_of * picker)
        fresh = (picker - jnp.dot(row_of, inverse, precision=lax.Precision.HIGHEST)) / pivot
        return inverse + picker[:, None] * fresh[None, :]

    return lax.fori_loop(0, order, row_step, jnp.zeros_like(lower))


def orthogonalize(tall_block, gram):
    lower = lower_factor(gram)
    inverse = lower_inverse(lower)
    result = jnp.dot(
        tall_block, inverse.T, precision=lax.Precision.HIGHEST, preferred_element_type=jnp.float32
    )
    return (result, lower.T)


def shards(displacement, velocity, slopes, stretch, moduli, buoyancy, probes):
    previous = displacement - time_step * velocity
    current = displacement
    stacked = jnp.concatenate([slopes, stretch[None], moduli], 0)
    near_values = extended(stacked, (("gx", 2), ("gy", 3)), 2)
    for moment in range(STEPS):
        padded = extended(current, (("gx", 2), ("gy", 3)), 4)
        gradients = gradient(padded, near_values[0], near_values[1], near_values[2])
        stress = stresses(gradients, near_values[3], near_values[4])
        pushes = buoyancy * forces(stress, slopes[0], slopes[1], stretch)
        following = 2.0 * current - previous + time_step**2 * pushes
        velocities = (following - previous) / (2.0 * time_step)
        sampled = velocities[:, ::2, ::2, ::2]
        half_x = sampled.shape[2]
        rearranged = jnp.transpose(sampled, (2, 0, 1, 3)).reshape(-1, sampled.shape[3])
        sketch_term = jnp.dot(
            rearranged,
            probes[moment],
            precision=lax.Precision.HIGHEST,
            preferred_element_type=jnp.float32,
        ).reshape(half_x, -1, probes.shape[2])
        reduced = lax.psum_scatter(sketch_term, "gy", scatter_dimension=1, tiled=True)
        sketch = reduced if moment == 0 else sketch + reduced
        previous, current = (current, following)
    tall_block = sketch.reshape(-1, sketch.shape[2])
    rows_total = tall_block.shape[0] * lax.axis_size("gx") * lax.axis_size("gy")
    gram_local = jnp.dot(
        tall_block.T,
        tall_block,
        precision=lax.Precision.HIGHEST,
        preferred_element_type=jnp.float32,
    )
    gram_whole = lax.psum(gram_local, ("gx", "gy"))
    orthonormal, factor = orthogonalize(tall_block, gram_whole)
    basis = (math.sqrt(rows_total) * orthonormal).reshape(sketch.shape)
    return (current, basis, factor)


def solution(mesh):
    in_specs = (
        P(None, None, "gx", "gy"),
        P(None, None, "gx", "gy"),
        P(None, None, "gx", "gy"),
        P(None, "gx", "gy"),
        P(None, None, "gx", "gy"),
        P(None, "gx", "gy"),
        P(None, "gy", None),
    )
    out_specs = (P(None, None, "gx", "gy"), P("gx", "gy", None), P())
    return jax.shard_map(shards, mesh=mesh, in_specs=in_specs, out_specs=out_specs, check_vma=False)
```

profile of v0, /device:TPU:1, one launch (start us, length us, event | category | flops | bytes accessed | tf_op | source)
XLA Modules:
  0.0 987.9 jit_solution(11689234760993657389)
XLA Ops:
  10.5 5.2 collective-permute-start
  18.5 4.9 collective-permute-start.4
  31.3 4.7 collective-permute-start.3
  44.7 4.6 pad_maximum_fusion
  63.1 3.5 fusion.87
  67.4 4.9 fusion.56
  79.5 3.9 collective-permute-start.8
  86.8 5.7 collective-permute-done.9
  92.8 3.6 collective-permute-start.11
  108.5 4.5 fusion.50
  123.0 6.1 collective-permute-start.12
  132.6 6.9 slice.1053
  152.7 6.9 slice.1055
  168.3 3.5 fusion.69
  172.6 4.9 fusion.44
  191.6 5.8 collective-permute-start.16
  199.1 6.9 slice.1057
  212.1 3.9 collective-permute-start.19
  228.2 4.9 fusion.38
  241.1 7.0 slice.1059
  250.0 7.7 reduce-scatter.2.cloned.1.call-done
  260.7 125.2 %all-reduce.10.cloned.1.call-done = f32[128,128]{1,0:T(8,128)} async-done(((f32[128,128]{1,0:T(8,128)}), f32[128,128]{1,0:T(8,128)}) %all-reduce.10.cloned.1.call-update) | async-done | bytes 65552 | tf_op jit(solution)/shard_map/psum | solution.py:154
  385.8 363.3 %while.30 = (s32[]{:T(128)}, f32[128,128]{1,0:T(8,128)S(1)}, f32[128,128]{1,0:T(8,128)}, s32[]{:T(128)}, s32[]{:T(128)}) while((s32[]{:T(128)}, f32[128,128]{1,0:T(8,128)S(1)}, f32[128,128]{1,0:T(8,128)}, s32[]{:T(128)}, s32[]{:T(128)}) %tuple.121), condition=%wide.region_7.8_spmd.clone.clone, body=%wide.region_5.7_spmd.clone.clone.sunk | while | flops 673410 | bytes 332917 | solution.py:96
  749.9 230.0 %while.29 = (s32[]{:T(128)}, f32[128,128]{1,0:T(8,128)S(1)}, f32[128,128]{1,0:T(8,128)S(1)}, s32[]{:T(128)}, s32[]{:T(128)}) while((s32[]{:T(128)}, f32[128,128]{1,0:T(8,128)S(1)}, f32[128,128]{1,0:T(8,128)S(1)}, s32[]{:T(128)}, s32[]{:T(128)}) %tuple.124), condition=%wide.region_10.11_spmd.clone, body=%wide.region_8.10_spmd.clone.sunk | while | flops 460034 | bytes 265316 | solution.py:110
  (1557 shorter events, 638.5 us)
Async XLA Ops:
  7.2 250.4 %reduce-scatter.2.cloned.1.call-start = ((), (), s32[]{:S(2)}) async-start(), calls=%async_computation.2 | async-start | bytes 147456 | tf_op jit(solution)/shard_map/reduce_scatter | solution.py:143
  9.2 17.0 %collective-permute-start.1 = (f32[5,32,2,128]{3,1,2,0:T(8,128)}, f32[5,32,2,128]{3,1,2,0:T(8,128)}, u32[]{:S(2)}, u32[]{:S(2)}) collective-permute-start(f32[5,32,2,128]{3,1,2,0:T(8,128)} %copy.382), channel_id=1, source_target_pairs={{2,0},{4,2},{6,4},{8,6},{10,8},{12,10},{14,12},{16,14},{18,16},{20... | collective-permute-start | bytes 491528 | tf_op jit(solution)/shard_map/ppermute | solution.py:19
  10.5 14.3 %collective-permute-start = (f32[5,32,2,128]{3,1,2,0:T(8,128)S(1)}, f32[5,32,2,128]{3,1,2,0:T(8,128)}, u32[]{:S(2)}, u32[]{:S(2)}) collective-permute-start(f32[5,32,2,128]{3,1,2,0:T(8,128)S(1)} %copy.381), channel_id=1, source_target_pairs={{0,2},{2,4},{4,6},{6,8},{8,10},{10,12},{12,14},{14,16},{16,18},{18... | collective-permute-start | bytes 491528 | tf_op jit(solution)/shard_map/ppermute | solution.py:16
  16.5 34.9 %collective-permute-start.5 = (f32[3,32,4,128]{3,1,2,0:T(8,128)}, f32[3,32,4,128]{3,1,2,0:T(8,128)}, u32[]{:S(2)}, u32[]{:S(2)}) collective-permute-start(f32[3,32,4,128]{3,1,2,0:T(8,128)} %copy.384), channel_id=1, source_target_pairs={{2,0},{4,2},{6,4},{8,6},{10,8},{12,10},{14,12},{16,14},{18,16},{20... | collective-permute-start | bytes 589832 | tf_op jit(solution)/shard_map/ppermute | solution.py:19
  18.5 30.8 %collective-permute-start.4 = (f32[3,32,4,128]{3,1,2,0:T(8,128)}, f32[3,32,4,128]{3,1,2,0:T(8,128)}, u32[]{:S(2)}, u32[]{:S(2)}) collective-permute-start(f32[3,32,4,128]{3,1,2,0:T(8,128)} %copy.383), channel_id=1, source_target_pairs={{0,2},{2,4},{4,6},{6,8},{8,10},{10,12},{12,14},{14,16},{16,18},{18... | collective-permute-start | bytes 589832 | tf_op jit(solution)/shard_map/ppermute | solution.py:16
  30.0 14.7 %collective-permute-start.2 = (f32[5,32,12,2]{1,3,2,0:T(2,128)}, f32[5,32,12,2]{1,3,2,0:T(2,128)}, u32[]{:S(2)}, u32[]{:S(2)}) collective-permute-start(f32[5,32,12,2]{1,3,2,0:T(2,128)} %get-tuple-element.285), channel_id=1, source_target_pairs={{0,1},{2,3},{4,5},{6,7},{8,9},{10,11},{12,13},{14,15},{16,17},{18,... | collective-permute-start | bytes 46088 | tf_op jit(solution)/shard_map/ppermute | solution.py:16
  31.3 13.4 %collective-permute-start.3 = (f32[5,32,12,2]{1,3,2,0:T(2,128)}, f32[5,32,12,2]{1,3,2,0:T(2,128)}, u32[]{:S(2)}, u32[]{:S(2)}) collective-permute-start(f32[5,32,12,2]{1,3,2,0:T(2,128)} %get-tuple-element.286), channel_id=1, source_target_pairs={{1,0},{3,2},{5,4},{7,6},{9,8},{11,10},{13,12},{15,14},{17,16},{19,... | collective-permute-start | bytes 46088 | tf_op jit(solution)/shard_map/ppermute | solution.py:19
  37.8 37.8 %copy-start.25 = (f32[32,8,128]{0,2,1:T(8,128)}, f32[32,8,128]{0,2,1:T(8,128)S(1)}, u32[]{:S(2)}) copy-start(f32[32,8,128]{0,2,1:T(8,128)S(1)} %copy.331) | copy-start | bytes 393220
  54.5 4.8 collective-permute-start.7
  55.9 3.4 collective-permute-start.6
  79.5 7.0 collective-permute-start.8
  83.6 8.8 collective-permute-start.9
  92.8 4.9 collective-permute-start.11
  96.4 3.2 collective-permute-start.10
  123.0 17.4 %collective-permute-start.12 = (f32[3,32,4,128]{3,1,2,0:T(8,128)}, f32[3,32,4,128]{3,1,2,0:T(8,128)}, u32[]{:S(2)}, u32[]{:S(2)}) collective-permute-start(f32[3,32,4,128]{3,1,2,0:T(8,128)} %copy.348), channel_id=1, source_target_pairs={{0,2},{2,4},{4,6},{6,8},{8,10},{10,12},{12,14},{14,16},{16,18},{18... | collective-permute-start | bytes 589832 | tf_op jit(solution)/shard_map/ppermute | solution.py:16
  131.1 11.3 %collective-permute-start.13 = (f32[3,32,4,128]{3,1,2,0:T(8,128)}, f32[3,32,4,128]{3,1,2,0:T(8,128)}, u32[]{:S(2)}, u32[]{:S(2)}) collective-permute-start(f32[3,32,4,128]{3,1,2,0:T(8,128)} %copy.349), channel_id=1, source_target_pairs={{2,0},{4,2},{6,4},{8,6},{10,8},{12,10},{14,12},{16,14},{18,16},{20... | collective-permute-start | bytes 589832 | tf_op jit(solution)/shard_map/ppermute | solution.py:19
  146.8 13.6 %collective-permute-start.15 = (f32[3,32,16,4]{1,2,3,0:T(8,128)}, f32[3,32,16,4]{1,2,3,0:T(8,128)}, u32[]{:S(2)}, u32[]{:S(2)}) collective-permute-start(f32[3,32,16,4]{1,2,3,0:T(8,128)} %copy.353), channel_id=1, source_target_pairs={{1,0},{3,2},{5,4},{7,6},{9,8},{11,10},{13,12},{15,14},{17,16},{19,... | collective-permute-start | bytes 73736 | tf_op jit(solution)/shard_map/ppermute | solution.py:19
  149.8 11.6 %collective-permute-start.14 = (f32[3,32,16,4]{1,2,3,0:T(8,128)}, f32[3,32,16,4]{1,2,3,0:T(8,128)}, u32[]{:S(2)}, u32[]{:S(2)}) collective-permute-start(f32[3,32,16,4]{1,2,3,0:T(8,128)} %copy.352), channel_id=1, source_target_pairs={{0,1},{2,3},{4,5},{6,7},{8,9},{10,11},{12,13},{14,15},{16,17},{18,... | collective-permute-start | bytes 73736 | tf_op jit(solution)/shard_map/ppermute | solution.py:16
  190.3 18.6 %collective-permute-start.17 = (f32[3,32,4,128]{3,1,2,0:T(8,128)}, f32[3,32,4,128]{3,1,2,0:T(8,128)}, u32[]{:S(2)}, u32[]{:S(2)}) collective-permute-start(f32[3,32,4,128]{3,1,2,0:T(8,128)} %copy.362), channel_id=1, source_target_pairs={{2,0},{4,2},{6,4},{8,6},{10,8},{12,10},{14,12},{16,14},{18,16},{20... | collective-permute-start | bytes 589832 | tf_op jit(solution)/shard_map/ppermute | solution.py:19
  191.6 15.2 %collective-permute-start.16 = (f32[3,32,4,128]{3,1,2,0:T(8,128)}, f32[3,32,4,128]{3,1,2,0:T(8,128)}, u32[]{:S(2)}, u32[]{:S(2)}) collective-permute-start(f32[3,32,4,128]{3,1,2,0:T(8,128)} %copy.361), channel_id=1, source_target_pairs={{0,2},{2,4},{4,6},{6,8},{8,10},{10,12},{12,14},{14,16},{16,18},{18... | collective-permute-start | bytes 589832 | tf_op jit(solution)/shard_map/ppermute | solution.py:16
  212.1 6.3 collective-permute-start.19
  216.1 3.2 collective-permute-start.18
  249.9 135.9 %all-reduce.10.cloned.1.call-start = ((), (), s32[]{:S(2)}) async-start(), calls=%async_computation.1 | async-start | bytes 131072 | tf_op jit(solution)/shard_map/psum | solution.py:154
  259.5 720.5 %copy-start.55 = (f32[4,24,128]{2,1,0:T(8,128)S(1)}, f32[4,24,128]{2,1,0:T(8,128)}, u32[]{:S(2)}) copy-start(f32[4,24,128]{2,1,0:T(8,128)} %reduce-scatter.2.cloned.1.call-done) | copy-start | bytes 147460
  (59 other events, 371.8 us)
Sparse Core Ops, SparseCore 0:
  250.0 7.5 reduce-scatter.1
  263.8 122.0 all-reduce.9
where the time goes:
time: 1000 us; the launch traced here: 988 us
  matrix products  478 us (48%)
  waiting for transfers between devices  142 us (14%)
  other arithmetic  116 us (12%)
  loops' own time  98.3 us (10%)
  local copies, waits for them, and re-layouts  81.5 us (8%)
  starting transfers between devices  56.2 us (6%)
  between operations  15.7 us (2%)
    psum x1, waiting for transfers between devices, shards(): gram_whole = lax.psum(gram_local, ('gx', 'gy'))  125 us
    dot_general x128, matrix products, column_step(): column = jnp.dot(gram, picker, precision=lax.Precision.HIGHEST)  124 us
    dot_general x128, matrix products, column_step(): column = column - jnp.dot(lower, row_of, precision=lax.Precision.HIGHEST)  108 us
    dot_general x128, matrix products, row_step(): jnp.dot(row_of, inverse, precision=lax.Precision.HIGHEST)  107 us
    dot_general x128, matrix products, row_step(): row_of = jnp.dot(picker, lower, precision=lax.Precision.HIGHEST)  105 us
    another operation x1, loops' own time, lower_factor(): return lax.fori_loop(0, order, column_step, jnp.zeros_like(gram))  94 us
    ppermute x10, starting transfers between devices, extended(): lax.ppermute(lax.slice_in_dim(block, block.shape[dim] - width, None, axis...  32.5 us
    div x8, other arithmetic, fourth(): return (segment(0) - segment(4) + 8.0 * (segment(3) - segment(1))) / 12.0  32.5 us
  transfers between devices with their start and end apart: 22, of which 6 were waited for; matrix products, arithmetic and copies ran while one was open for 6% of the time, Pallas kernels for 0%

commit v1 on v0

--- a/solution.py
+++ b/solution.py
@@ -151,7 +151,7 @@
         precision=lax.Precision.HIGHEST,
         preferred_element_type=jnp.float32,
     )
-    gram_whole = lax.psum(gram_local, ("gx", "gy"))
+    gram_whole = jnp.sum(lax.all_gather(gram_local, ("gx", "gy")), axis=0)
     orthonormal, factor = orthogonalize(tall_block, gram_whole)
     basis = (math.sqrt(rows_total) * orthonormal).reshape(sketch.shape)
     return (current, basis, factor)

time: 1000 us -> 823 us (0.82)
  matrix products: 478 us -> 370 us
  waiting for transfers between devices: 142 us -> 75 us
    psum x1 -> x0, waiting for transfers between devices: 125 us -> none  [shards(): gram_whole = lax.psum(gram_local, ('gx', 'gy'))]
    dot_general x128, matrix products: 124 us -> 16.4 us  [column_step(): column = jnp.dot(gram, picker, precision=lax.Precision.HIGHEST)]
    all_gather x0 -> x1, waiting for transfers between devices: none -> 57.8 us  [shards(): gram_whole = jnp.sum(lax.all_gather(gram_local, ('gx', 'gy')), axis=0)]
  transfers between devices with their start and end apart: 22 -> 22, of which waited for: 6 -> 6; matrix products, arithmetic and copies ran while one was open for 6% -> 8% of each run, Pallas kernels for 0% -> 0%
where the time goes in v1:
time: 823 us; the launch traced here: 815 us
  matrix products  370 us (45%)
  other arithmetic  118 us (14%)
  loops' own time  98.3 us (12%)
  local copies, waits for them, and re-layouts  81.5 us (10%)
  waiting for transfers between devices  75 us (9%)
  starting transfers between devices  56.2 us (7%)
  between operations  15.7 us (2%)
    dot_general x128, matrix products, column_step(): column = column - jnp.dot(lower, row_of, precision=lax.Precision.HIGHEST)  108 us
    dot_general x128, matrix products, row_step(): jnp.dot(row_of, inverse, precision=lax.Precision.HIGHEST)  107 us
    dot_general x128, matrix products, row_step(): row_of = jnp.dot(picker, lower, precision=lax.Precision.HIGHEST)  105 us
    another operation x1, loops' own time, lower_factor(): return lax.fori_loop(0, order, column_step, jnp.zeros_like(gram))  94 us
    all_gather x1, waiting for transfers between devices, shards(): gram_whole = jnp.sum(lax.all_gather(gram_local, ('gx', 'gy')), axis=0)  57.8 us
    ppermute x10, starting transfers between devices, extended(): lax.ppermute(lax.slice_in_dim(block, block.shape[dim] - width, None, axis...  32.5 us
    div x8, other arithmetic, fourth(): return (segment(0) - segment(4) + 8.0 * (segment(3) - segment(1))) / 12.0  32.5 us
    slice x4, local copies, waits for them, and re-layouts, shards(): sampled = velocities[:, ::2, ::2, ::2]  27.8 us
  transfers between devices with their start and end apart: 22, of which 6 were waited for; matrix products, arithmetic and copies ran while one was open for 8% of the time, Pallas kernels for 0%

profile of v1, /device:TPU:1, one launch (start us, length us, event | category | flops | bytes accessed | tf_op | source)
XLA Modules:
  0.0 814.7 jit_solution(13030031870366113874)
XLA Ops:
  10.5 5.2 collective-permute-start
  18.5 4.9 collective-permute-start.4
  31.3 4.7 collective-permute-start.3
  44.7 4.6 pad_maximum_fusion
  63.1 3.5 fusion.87
  67.4 4.9 fusion.56
  79.5 3.9 collective-permute-start.8
  86.8 5.7 collective-permute-done.9
  92.8 3.6 collective-permute-start.11
  108.5 4.5 fusion.50
  123.0 6.1 collective-permute-start.12
  132.6 6.9 slice.1053
  152.7 6.9 slice.1055
  168.3 3.5 fusion.69
  172.6 4.9 fusion.44
  191.6 5.8 collective-permute-start.16
  199.1 6.9 slice.1057
  212.1 3.9 collective-permute-start.19
  228.2 4.9 fusion.38
  241.1 7.0 slice.1059
  250.0 7.7 reduce-scatter.2.cloned.1.call-done
  260.7 57.8 %all-gather.3.cloned.1.call-done = f32[4096,128]{1,0:T(8,128)} async-done(((f32[128,128]{1,0:T(8,128)}), f32[4096,128]{1,0:T(8,128)}) %all-gather.3.cloned.1.call-update) | async-done | bytes 2097168 | tf_op jit(solution)/shard_map/all_gather | solution.py:154
  320.2 255.8 %while.30 = (s32[]{:T(128)}, f32[128,128]{1,0:T(8,128)S(1)}, f32[128,128]{1,0:T(8,128)S(1)}, s32[]{:T(128)}, s32[]{:T(128)}) while((s32[]{:T(128)}, f32[128,128]{1,0:T(8,128)S(1)}, f32[128,128]{1,0:T(8,128)S(1)}, s32[]{:T(128)}, s32[]{:T(128)}) %tuple.121), condition=%wide.region_7.8_spmd.clone.clone, body=%wide.region_5.7_spmd.clone.clone.sunk | while | flops 673410 | bytes 332917 | solution.py:96
  576.7 230.0 %while.29 = (s32[]{:T(128)}, f32[128,128]{1,0:T(8,128)S(1)}, f32[128,128]{1,0:T(8,128)S(1)}, s32[]{:T(128)}, s32[]{:T(128)}) while((s32[]{:T(128)}, f32[128,128]{1,0:T(8,128)S(1)}, f32[128,128]{1,0:T(8,128)S(1)}, s32[]{:T(128)}, s32[]{:T(128)}) %tuple.124), condition=%wide.region_10.11_spmd.clone, body=%wide.region_8.10_spmd.clone.sunk | while | flops 460034 | bytes 265316 | solution.py:110
  (1558 shorter events, 532.7 us)
Async XLA Ops:
  7.2 250.5 %reduce-scatter.2.cloned.1.call-start = ((), (), s32[]{:S(2)}) async-start(), calls=%async_computation.2 | async-start | bytes 147456 | tf_op jit(solution)/shard_map/reduce_scatter | solution.py:143
  9.2 17.0 %collective-permute-start.1 = (f32[5,32,2,128]{3,1,2,0:T(8,128)}, f32[5,32,2,128]{3,1,2,0:T(8,128)}, u32[]{:S(2)}, u32[]{:S(2)}) collective-permute-start(f32[5,32,2,128]{3,1,2,0:T(8,128)} %copy.382), channel_id=1, source_target_pairs={{2,0},{4,2},{6,4},{8,6},{10,8},{12,10},{14,12},{16,14},{18,16},{20... | collective-permute-start | bytes 491528 | tf_op jit(solution)/shard_map/ppermute | solution.py:19
  10.5 14.3 %collective-permute-start = (f32[5,32,2,128]{3,1,2,0:T(8,128)S(1)}, f32[5,32,2,128]{3,1,2,0:T(8,128)}, u32[]{:S(2)}, u32[]{:S(2)}) collective-permute-start(f32[5,32,2,128]{3,1,2,0:T(8,128)S(1)} %copy.381), channel_id=1, source_target_pairs={{0,2},{2,4},{4,6},{6,8},{8,10},{10,12},{12,14},{14,16},{16,18},{18... | collective-permute-start | bytes 491528 | tf_op jit(solution)/shard_map/ppermute | solution.py:16
  16.5 34.9 %collective-permute-start.5 = (f32[3,32,4,128]{3,1,2,0:T(8,128)}, f32[3,32,4,128]{3,1,2,0:T(8,128)}, u32[]{:S(2)}, u32[]{:S(2)}) collective-permute-start(f32[3,32,4,128]{3,1,2,0:T(8,128)} %copy.384), channel_id=1, source_target_pairs={{2,0},{4,2},{6,4},{8,6},{10,8},{12,10},{14,12},{16,14},{18,16},{20... | collective-permute-start | bytes 589832 | tf_op jit(solution)/shard_map/ppermute | solution.py:19
  18.5 30.8 %collective-permute-start.4 = (f32[3,32,4,128]{3,1,2,0:T(8,128)}, f32[3,32,4,128]{3,1,2,0:T(8,128)}, u32[]{:S(2)}, u32[]{:S(2)}) collective-permute-start(f32[3,32,4,128]{3,1,2,0:T(8,128)} %copy.383), channel_id=1, source_target_pairs={{0,2},{2,4},{4,6},{6,8},{8,10},{10,12},{12,14},{14,16},{16,18},{18... | collective-permute-start | bytes 589832 | tf_op jit(solution)/shard_map/ppermute | solution.py:16
  30.0 14.7 %collective-permute-start.2 = (f32[5,32,12,2]{1,3,2,0:T(2,128)}, f32[5,32,12,2]{1,3,2,0:T(2,128)}, u32[]{:S(2)}, u32[]{:S(2)}) collective-permute-start(f32[5,32,12,2]{1,3,2,0:T(2,128)} %get-tuple-element.285), channel_id=1, source_target_pairs={{0,1},{2,3},{4,5},{6,7},{8,9},{10,11},{12,13},{14,15},{16,17},{18,... | collective-permute-start | bytes 46088 | tf_op jit(solution)/shard_map/ppermute | solution.py:16
  31.3 13.4 %collective-permute-start.3 = (f32[5,32,12,2]{1,3,2,0:T(2,128)}, f32[5,32,12,2]{1,3,2,0:T(2,128)}, u32[]{:S(2)}, u32[]{:S(2)}) collective-permute-start(f32[5,32,12,2]{1,3,2,0:T(2,128)} %get-tuple-element.286), channel_id=1, source_target_pairs={{1,0},{3,2},{5,4},{7,6},{9,8},{11,10},{13,12},{15,14},{17,16},{19,... | collective-permute-start | bytes 46088 | tf_op jit(solution)/shard_map/ppermute | solution.py:19
  37.8 37.8 %copy-start.25 = (f32[32,8,128]{0,2,1:T(8,128)}, f32[32,8,128]{0,2,1:T(8,128)S(1)}, u32[]{:S(2)}) copy-start(f32[32,8,128]{0,2,1:T(8,128)S(1)} %copy.331) | copy-start | bytes 393220
  54.5 4.8 collective-permute-start.7
  55.9 3.4 collective-permute-start.6
  79.5 7.0 collective-permute-start.8
  83.6 8.8 %collective-permute-start.9 = (f32[3,32,4,128]{3,1,2,0:T(8,128)S(1)}, f32[3,32,4,128]{3,1,2,0:T(8,128)S(1)}, u32[]{:S(2)}, u32[]{:S(2)}) collective-permute-start(f32[3,32,4,128]{3,1,2,0:T(8,128)S(1)} %copy.336), channel_id=1, source_target_pairs={{2,0},{4,2},{6,4},{8,6},{10,8},{12,10},{14,12},{16,14},{18,16},{20... | collective-permute-start | bytes 589832 | tf_op jit(solution)/shard_map/ppermute | solution.py:19
  92.8 4.9 collective-permute-start.11
  96.4 3.2 collective-permute-start.10
  123.0 17.4 %collective-permute-start.12 = (f32[3,32,4,128]{3,1,2,0:T(8,128)}, f32[3,32,4,128]{3,1,2,0:T(8,128)}, u32[]{:S(2)}, u32[]{:S(2)}) collective-permute-start(f32[3,32,4,128]{3,1,2,0:T(8,128)} %copy.348), channel_id=1, source_target_pairs={{0,2},{2,4},{4,6},{6,8},{8,10},{10,12},{12,14},{14,16},{16,18},{18... | collective-permute-start | bytes 589832 | tf_op jit(solution)/shard_map/ppermute | solution.py:16
  131.1 11.3 %collective-permute-start.13 = (f32[3,32,4,128]{3,1,2,0:T(8,128)}, f32[3,32,4,128]{3,1,2,0:T(8,128)}, u32[]{:S(2)}, u32[]{:S(2)}) collective-permute-start(f32[3,32,4,128]{3,1,2,0:T(8,128)} %copy.349), channel_id=1, source_target_pairs={{2,0},{4,2},{6,4},{8,6},{10,8},{12,10},{14,12},{16,14},{18,16},{20... | collective-permute-start | bytes 589832 | tf_op jit(solution)/shard_map/ppermute | solution.py:19
  146.8 13.6 %collective-permute-start.15 = (f32[3,32,16,4]{1,2,3,0:T(8,128)}, f32[3,32,16,4]{1,2,3,0:T(8,128)}, u32[]{:S(2)}, u32[]{:S(2)}) collective-permute-start(f32[3,32,16,4]{1,2,3,0:T(8,128)} %copy.353), channel_id=1, source_target_pairs={{1,0},{3,2},{5,4},{7,6},{9,8},{11,10},{13,12},{15,14},{17,16},{19,... | collective-permute-start | bytes 73736 | tf_op jit(solution)/shard_map/ppermute | solution.py:19
  149.8 11.6 %collective-permute-start.14 = (f32[3,32,16,4]{1,2,3,0:T(8,128)}, f32[3,32,16,4]{1,2,3,0:T(8,128)}, u32[]{:S(2)}, u32[]{:S(2)}) collective-permute-start(f32[3,32,16,4]{1,2,3,0:T(8,128)} %copy.352), channel_id=1, source_target_pairs={{0,1},{2,3},{4,5},{6,7},{8,9},{10,11},{12,13},{14,15},{16,17},{18,... | collective-permute-start | bytes 73736 | tf_op jit(solution)/shard_map/ppermute | solution.py:16
  190.3 18.6 %collective-permute-start.17 = (f32[3,32,4,128]{3,1,2,0:T(8,128)}, f32[3,32,4,128]{3,1,2,0:T(8,128)}, u32[]{:S(2)}, u32[]{:S(2)}) collective-permute-start(f32[3,32,4,128]{3,1,2,0:T(8,128)} %copy.362), channel_id=1, source_target_pairs={{2,0},{4,2},{6,4},{8,6},{10,8},{12,10},{14,12},{16,14},{18,16},{20... | collective-permute-start | bytes 589832 | tf_op jit(solution)/shard_map/ppermute | solution.py:19
  191.6 15.2 %collective-permute-start.16 = (f32[3,32,4,128]{3,1,2,0:T(8,128)}, f32[3,32,4,128]{3,1,2,0:T(8,128)}, u32[]{:S(2)}, u32[]{:S(2)}) collective-permute-start(f32[3,32,4,128]{3,1,2,0:T(8,128)} %copy.361), channel_id=1, source_target_pairs={{0,2},{2,4},{4,6},{6,8},{8,10},{10,12},{12,14},{14,16},{16,18},{18... | collective-permute-start | bytes 589832 | tf_op jit(solution)/shard_map/ppermute | solution.py:16
  212.1 6.3 collective-permute-start.19
  216.1 3.2 collective-permute-start.18
  249.9 68.5 %all-gather.3.cloned.1.call-start = ((), (), s32[]{:S(2)}) async-start(), calls=%async_computation.1 | async-start | bytes 2162688 | tf_op jit(solution)/shard_map/all_gather | solution.py:154
  318.5 488.3 %copy-start.55 = (f32[4,24,128]{2,1,0:T(8,128)S(1)}, f32[4,24,128]{2,1,0:T(8,128)}, u32[]{:S(2)}) copy-start(f32[4,24,128]{2,1,0:T(8,128)} %reduce-scatter.2.cloned.1.call-done) | copy-start | bytes 147460
  (59 other events, 371.8 us)
Sparse Core Ops, SparseCore 0:
  250.0 7.5 reduce-scatter.1
  261.1 57.3 all-gather.2
